TPU v7x, 32 devices: a whole 2x2x4 slice. The times are simulated.
32 devices in a mesh: mp: 8 (over z, y), dp: 4 (over x, core).
Axes of the slice: x: 2, y: 2, z: 4, core: 2. Of those that a mesh axis runs over, the one named last changes fastest.
Arguments:
- forward_fields: bfloat16 [16, 4, 16384], P(None, None, 'mp'), may hold values from -6 to 6
- adjoint_fields: bfloat16 [64, 4, 16384], P(None, None, 'mp'), may hold values from -6 to 6
- data_rec: int32 [768], P('dp'), may hold values from 0 to 63
- data_freq: int32 [768], P('dp'), may hold values from 0 to 15
- data_coef: float32 [768, 4], P('dp'), may hold values from -6 to 6
- residual_cols: bfloat16 [768, 256], P('dp'), may hold values from -6 to 6
Outputs:
- data_update: bfloat16 [768, 256], P('dp')
- model_update: float32 [16384, 256], P(('mp', 'dp'))
All inputs are finite; a program needn't handle non-finite values.
Results may differ from a plain program's by a relative error of at most 0.0075.
Values may be sent and summed in bfloat16 or wider, within the bound.
A program may use at most 64 MiB of HBM per device.

v0:
```python
import math
import jax
import jax.numpy as jnp
from jax import lax
from jax.sharding import PartitionSpec as P

GRID_COLS = 128
SWEEPS = 2


def with_halo(array, sides, width):
    for axis, dim in sides:
        peers, length = (lax.axis_size(axis), array.shape[dim])
        up = [(i, (i + 1) % peers) for i in range(peers - 1)]
        down = [(j, i) for i, j in up]
        last = lax.slice_in_dim(array, length - width, length, axis=dim)
        leading = lax.slice_in_dim(array, 0, width, axis=dim)
        before = lax.ppermute(last, axis, up)
        after = lax.ppermute(leading, axis, down)
        array = jnp.concatenate([before, array, after], axis=dim)
    return array


def sweep_once(field):
    center = field[:, 1:-1, :]
    sides = jnp.pad(center, ((0, 0), (0, 0), (1, 1)))
    beside_all = field[:, :-2, :] + field[:, 2:, :] + sides[:, :, :-2] + sides[:, :, 2:]
    return center + 0.2 * (beside_all - 4.0 * center)


def per_device(forward_fields, adjoint_fields, data_rec, data_freq, data_coef, residual_cols):
    rows_here = data_rec.shape[0]
    cells_here = forward_fields.shape[2]
    slab_rows = cells_here // GRID_COLS
    slab_count = lax.axis_size("mp")
    block_count = lax.axis_size("dp")
    adjoint = adjoint_fields[data_rec].astype(jnp.float32)
    forward = forward_fields[data_freq].astype(jnp.float32)
    sens = (0.5 * jnp.sum(data_coef[:, :, None] * adjoint * forward, axis=1)).astype(jnp.bfloat16)
    grid = sens.astype(jnp.float32).reshape(rows_here, slab_rows, GRID_COLS)
    extended = with_halo(grid.astype(jnp.bfloat16), (("mp", 1),), SWEEPS).astype(grid.dtype)
    first_row = lax.axis_index("mp") * slab_rows
    total_rows = slab_rows * slab_count
    for sweep in range(SWEEPS):
        extended = sweep_once(extended)
        margin = SWEEPS - 1 - sweep
        if margin > 0:
            global_rows = first_row - margin + jnp.arange(slab_rows + 2 * margin, dtype=jnp.int32)
            inside = (global_rows >= 0) & (global_rows < total_rows)
            extended = jnp.where(inside[None, :, None], extended, 0.0)
    grid = extended
    smooth = grid.reshape(rows_here, cells_here).astype(jnp.bfloat16)
    residual_whole = lax.all_gather(residual_cols, "dp", axis=0, tiled=True)
    gram_tile = lax.dot_general(
        smooth,
        lax.all_gather(sens, "dp", axis=0, tiled=True),
        (((1,), (1,)), ((), ())),
        preferred_element_type=jnp.float32,
    )
    partial_value = jnp.dot(
        gram_tile, residual_whole.astype(jnp.float32), precision=lax.Precision.HIGHEST
    )
    gram_prod = lax.psum(partial_value, "mp") / (cells_here * slab_count)
    data_update = (gram_prod + residual_cols.astype(jnp.float32)).astype(jnp.bfloat16)
    summed = lax.psum_scatter(
        lax.dot_general(
            smooth, data_update, (((0,), (0,)), ((), ())), preferred_element_type=jnp.float32
        ),
        "dp",
        scatter_dimension=0,
        tiled=True,
    )
    model_update = summed / math.sqrt(rows_here * block_count)
    return (data_update, model_update)


def solution(mesh):
    in_specs = (
        P(None, None, "mp"),
        P(None, None, "mp"),
        P("dp"),
        P("dp"),
        P("dp", None),
        P("dp", None),
    )
    out_specs = (P("dp", None), P(("mp", "dp"), None))
    return jax.shard_map(
        per_device, mesh=mesh, in_specs=in_specs, out_specs=out_specs, check_vma=False
    )
```

profile of v0, /device:TPU:0, one launch (start us, length us, event | category | flops | bytes accessed | tf_op | source)
XLA Modules:
  0.0 189.3 jit_solution(5085543405692865950)
XLA Ops:
  7.2 0.0 copy-start
  7.2 0.0 all-gather.2.cloned.1.call-start
  7.2 0.8 compare_select_fusion.1
  8.0 0.7 compare_select_fusion
  8.7 0.8 copy.10
  9.5 0.0 copy-done
  9.5 0.0 copy-start.1
  9.5 9.6 %gather_fusion = bf16[192,4,2048]{2,1,0:T(4,128)(2,1)} fusion(bf16[64,4,2048]{2,1,0:T(4,128)(2,1)S(1)} %copy-done, s32[1024]{0:T(1024)S(1)} %pad_clamp_fusion.1), kind=kCustom, calls=%fused_computation | custom fusion | bytes 6292224 | tf_op jit(solution)/shard_map/gather | solution.py:37
  19.1 0.0 copy-done.1
  19.1 9.7 %gather_fusion.1 = bf16[192,4,2048]{2,1,0:T(4,128)(2,1)} fusion(bf16[16,4,2048]{2,1,0:T(4,128)(2,1)S(1)} %copy-done.1, s32[1024]{0:T(1024)S(1)} %pad_clamp_fusion), kind=kCustom, calls=%fused_computation.1 | custom fusion | bytes 6292224 | tf_op jit(solution)/shard_map/gather | solution.py:38
  28.8 9.7 %multiply_reduce_fusion = f32[192,2048]{1,0:T(8,128)S(1)} fusion(bf16[192,4,2048]{2,1,0:T(4,128)(2,1)} %gather_fusion.1, bf16[192,4,2048]{2,1,0:T(4,128)(2,1)} %gather_fusion, f32[192,4]{1,0:T(8,128)S(1)} %copy.10), kind=kLoop, calls=%fused_computation.2 | loop fusion | flops 7471104 | bytes 7867392 | tf_op jit(solution)/shard_map/reduce_sum | solution.py:39
  38.5 0.0 copy-start.3
  38.5 1.0 multiply_convert_fusion
  39.5 0.0 all-gather.2.cloned.1.call-update
  39.5 0.0 all-reduce.4.cloned.1.call-start
  39.6 1.4 copy.14
  41.0 4.9 %collective-permute-start = (bf16[192,2,128]{0,2,1:T(8,128)(2,1)S(1)}, bf16[192,2,128]{0,2,1:T(8,128)(2,1)S(1)}, u32[]{:S(2)}, u32[]{:S(2)}) collective-permute-start(bf16[192,2,128]{0,2,1:T(8,128)(2,1)S(1)} %get-tuple-element.2), channel_id=1, source_target_pairs={{0,4},{4,8},{8,12},{12,16},{16,20},{20,24},{24,28},{1,5},{5,9},{9,... | collective-permute-start | bytes 294920 | tf_op jit(solution)/shard_map/ppermute | solution.py:18
  46.0 1.3 collective-permute-start.1
  47.3 0.0 copy-done.3
  47.3 7.1 %all_gather.7 = bf16[768,256]{1,0:T(8,128)(2,1)S(1)} all-gather(bf16[192,256]{1,0:T(8,128)(2,1)S(1)} %copy-done.3), channel_id=1, replica_groups=mesh['mp'=8,'dp'=4] {'dp'}, dimensions={0}, use_global_device_ids=true | all-gather | bytes 491520 | tf_op jit(solution)/shard_map/all_gather | solution.py:53
  54.4 0.0 collective-permute-done
  54.4 0.0 collective-permute-done.1
  54.4 0.3 maximum_convert_fusion
  54.7 0.2 slice.54
  54.9 1.0 fusion.5
  55.9 0.1 slice.57
  56.1 0.8 fusion.11
  56.9 14.4 %all-gather.2.cloned.1.call-done = bf16[768,2048]{1,0:T(8,128)(2,1)} async-done(((bf16[192,2048]{1,0:T(8,128)(2,1)}), bf16[768,2048]{1,0:T(8,128)(2,1)}) %all-gather.2.cloned.1.call-update) | async-done | bytes 3145744 | tf_op jit(solution)/shard_map/all_gather | solution.py:56
  71.3 3.1 %fusion.13 = f32[192,768]{1,0:T(8,128)S(1)} fusion(bf16[192,2048]{0,1:T(8,128)(2,1)S(1)} %bitcast.10, bf16[768,2048]{1,0:T(8,128)(2,1)} %all-gather.2.cloned.1.call-done), kind=kOutput, calls=%fused_computation.31 | convolution fusion | flops 603979776 | bytes 4521984 | tf_op jit(solution)/shard_map/dot_general | solution.py:54
  74.4 1.1 fusion.14
  75.5 0.0 all-reduce.4.cloned.1.call-update
  75.5 0.0 reduce-scatter.2.cloned.1.call-start
  75.6 72.2 %all-reduce.4.cloned.1.call-done = f32[192,256]{1,0:T(8,128)} async-done(((f32[192,256]{1,0:T(8,128)}), f32[192,256]{1,0:T(8,128)}) %all-reduce.4.cloned.1.call-update) | async-done | bytes 196624 | tf_op jit(solution)/shard_map/psum | solution.py:63
  147.8 1.0 add_convert_fusion
  148.7 0.0 copy-start.2
  148.7 1.8 fusion.15
  150.5 0.0 reduce-scatter.2.cloned.1.call-update
  150.5 0.0 copy-done.2
  150.5 30.3 %reduce-scatter.2.cloned.1.call-done = f32[512,256]{1,0:T(8,128)} async-done(((f32[2048,256]{1,0:T(8,128)}), f32[512,256]{1,0:T(8,128)}) %reduce-scatter.2.cloned.1.call-update) | async-done | bytes 524304 | tf_op jit(solution)/shard_map/reduce_scatter | solution.py:65
  180.9 1.9 broadcast_multiply_fusion
  (4 shorter events, 0.0 us)
Async XLA Ops:
  7.2 2.3 %copy-start = (bf16[64,4,2048]{2,1,0:T(4,128)(2,1)S(1)}, bf16[64,4,2048]{2,1,0:T(4,128)(2,1)}, u32[]{:S(2)}) copy-start(bf16[64,4,2048]{2,1,0:T(4,128)(2,1)} %param.7) | copy-start | bytes 3145732
  7.2 64.1 %all-gather.2.cloned.1.call-start = ((), (), s32[]{:S(2)}) async-start(), calls=%async_computation.1 | async-start | bytes 3932160 | tf_op jit(solution)/shard_map/all_gather | solution.py:56
  9.5 9.6 %copy-start.1 = (bf16[16,4,2048]{2,1,0:T(4,128)(2,1)S(1)}, bf16[16,4,2048]{2,1,0:T(4,128)(2,1)}, u32[]{:S(2)}) copy-start(bf16[16,4,2048]{2,1,0:T(4,128)(2,1)} %param.6) | copy-start | bytes 786436
  38.5 8.8 %copy-start.3 = (bf16[192,256]{1,0:T(8,128)(2,1)S(1)}, bf16[192,256]{1,0:T(8,128)(2,1)}, u32[]{:S(2)}) copy-start(bf16[192,256]{1,0:T(8,128)(2,1)} %param.11) | copy-start | bytes 294916
  39.5 108.3 %all-reduce.4.cloned.1.call-start = ((), (), s32[]{:S(2)}) async-start(), calls=%async_computation.2 | async-start | bytes 393216 | tf_op jit(solution)/shard_map/psum | solution.py:63
  41.0 13.3 %collective-permute-start = (bf16[192,2,128]{0,2,1:T(8,128)(2,1)S(1)}, bf16[192,2,128]{0,2,1:T(8,128)(2,1)S(1)}, u32[]{:S(2)}, u32[]{:S(2)}) collective-permute-start(bf16[192,2,128]{0,2,1:T(8,128)(2,1)S(1)} %get-tuple-element.2), channel_id=1, source_target_pairs={{0,4},{4,8},{8,12},{12,16},{16,20},{20,24},{24,28},{1,5},{5,9},{9,... | collective-permute-start | bytes 294920 | tf_op jit(solution)/shard_map/ppermute | solution.py:18
  46.0 8.4 %collective-permute-start.1 = (bf16[192,2,128]{0,2,1:T(8,128)(2,1)S(1)}, bf16[192,2,128]{0,2,1:T(8,128)(2,1)S(1)}, u32[]{:S(2)}, u32[]{:S(2)}) collective-permute-start(bf16[192,2,128]{0,2,1:T(8,128)(2,1)S(1)} %get-tuple-element.3), channel_id=1, source_target_pairs={{4,0},{8,4},{12,8},{16,12},{20,16},{24,20},{28,24},{5,1},{9,5},{13... | collective-permute-start | bytes 294920 | tf_op jit(solution)/shard_map/ppermute | solution.py:19
  75.5 105.4 %reduce-scatter.2.cloned.1.call-start = ((), (), s32[]{:S(2)}) async-start(), calls=%async_computation.3 | async-start | bytes 2621440 | tf_op jit(solution)/shard_map/reduce_scatter | solution.py:65
  148.7 1.8 copy-start.2
Sparse Core Ops, SparseCore 0:
  39.6 31.6 all-gather.1
  75.7 72.0 all-reduce.3
  150.7 30.1 reduce-scatter.1
where the time goes:
time: 190 us; the launch traced here: 189 us
  waiting for transfers between devices  117 us (62%)
  local copies, waits for them, and re-layouts  21.9 us (12%)
  other arithmetic  17.1 us (9%)
  between operations  13.9 us (7%)
  blocking collectives  7.1 us (4%)
  starting transfers between devices  6.32 us (3%)
  matrix products  5.98 us (3%)
    psum x1, waiting for transfers between devices, per_device(): gram_prod = lax.psum(partial_value, 'mp') / (cells_here * slab_count)  72.2 us
    reduce_scatter x1, waiting for transfers between devices, per_device(): lax.psum_scatter(lax.dot_general(smooth, data_update, (((0,), (0,)), ((),...  30.3 us
    all_gather x1, waiting for transfers between devices, per_device(): lax.all_gather(sens, 'dp', axis=0, tiled=True)  14.4 us
    gather x1, local copies, waits for them, and re-layouts, per_device(): forward = forward_fields[data_freq].astype(jnp.float32)  9.69 us
    reduce_sum x1, other arithmetic, per_device(): jnp.sum(data_coef[:, :, None] * adjoint * forward, axis=1)  9.66 us
    gather x1, local copies, waits for them, and re-layouts, per_device(): adjoint = adjoint_fields[data_rec].astype(jnp.float32)  9.62 us
    all_gather x1, blocking collectives, per_device(): residual_whole = lax.all_gather(residual_cols, 'dp', axis=0, tiled=True)  7.1 us
    ppermute x1, starting transfers between devices, with_halo(): before = lax.ppermute(last, axis, up)  4.91 us
  transfers between devices with their start and end apart: 5, of which 3 were waited for; matrix products, arithmetic and copies ran while one was open for 2% of the time, Pallas kernels for 0%

commit v1 on v0

--- a/solution.py
+++ b/solution.py
@@ -3,6 +3,7 @@
 import jax.numpy as jnp
 from jax import lax
 from jax.sharding import PartitionSpec as P
+from jax.lax import all_gather
 
 GRID_COLS = 128
 SWEEPS = 2
@@ -60,7 +61,11 @@
     partial_value = jnp.dot(
         gram_tile, residual_whole.astype(jnp.float32), precision=lax.Precision.HIGHEST
     )
-    gram_prod = lax.psum(partial_value, "mp") / (cells_here * slab_count)
+
+    def fit_signs(u_in, link_axis):
+        return jnp.sum(all_gather(u_in, link_axis), axis=0)
+
+    gram_prod = fit_signs(partial_value, "mp") / (cells_here * slab_count)
     data_update = (gram_prod + residual_cols.astype(jnp.float32)).astype(jnp.bfloat16)
     summed = lax.psum_scatter(
         lax.dot_general(

time: 190 us -> 163 us (0.86)
  waiting for transfers between devices: 117 us -> 89.8 us
    psum x1 -> x0, waiting for transfers between devices: 72.2 us -> none  [per_device(): gram_prod = lax.psum(partial_value, 'mp') / (cells_here * slab_count)]
    all_gather x0 -> x1, waiting for transfers between devices: none -> 45.7 us  [fit_signs(): return jnp.sum(all_gather(u_in, link_axis), axis=0)]
where the time goes in v1:
time: 163 us
  waiting for transfers between devices  89.8 us (55%)
  local copies, waits for them, and re-layouts  21.9 us (13%)
  other arithmetic  17.7 us (11%)
  between operations  13.9 us (9%)
  blocking collectives  7.1 us (4%)
  starting transfers between devices  6.32 us (4%)
  matrix products  5.99 us (4%)
    all_gather x1, waiting for transfers between devices, fit_signs(): return jnp.sum(all_gather(u_in, link_axis), axis=0)  45.7 us
    reduce_scatter x1, waiting for transfers between devices, per_device(): lax.psum_scatter(lax.dot_general(smooth, data_update, (((0,), (0,)), ((),...  29.7 us
    all_gather x1, waiting for transfers between devices, per_device(): lax.all_gather(sens, 'dp', axis=0, tiled=True)  14.4 us
    gather x1, local copies, waits for them, and re-layouts, per_device(): forward = forward_fields[data_freq].astype(jnp.float32)  9.69 us
    reduce_sum x1, other arithmetic, per_device(): jnp.sum(data_coef[:, :, None] * adjoint * forward, axis=1)  9.66 us
    gather x1, local copies, waits for them, and re-layouts, per_device(): adjoint = adjoint_fields[data_rec].astype(jnp.float32)  9.62 us
    all_gather x1, blocking collectives, per_device(): residual_whole = lax.all_gather(residual_cols, 'dp', axis=0, tiled=True)  7.1 us
    ppermute x1, starting transfers between devices, with_halo(): before = lax.ppermute(last, axis, up)  4.91 us
  transfers between devices with their start and end apart: 5, of which 3 were waited for; matrix products, arithmetic and copies ran while one was open for 2% of the time, Pallas kernels for 0%

profile of v1, /device:TPU:0, one launch (start us, length us, event | category | flops | bytes accessed | tf_op | source)
XLA Modules:
  0.0 162.8 jit_solution(4962106662269690026)
XLA Ops:
  7.2 0.0 copy-start
  7.2 0.0 all-gather.4.cloned.1.call-start
  7.2 0.8 compare_select_fusion.1
  8.0 0.7 compare_select_fusion
  8.7 0.8 copy.10
  9.5 0.0 copy-done
  9.5 0.0 copy-start.1
  9.5 9.6 %gather_fusion = bf16[192,4,2048]{2,1,0:T(4,128)(2,1)} fusion(bf16[64,4,2048]{2,1,0:T(4,128)(2,1)S(1)} %copy-done, s32[1024]{0:T(1024)S(1)} %pad_clamp_fusion.1), kind=kCustom, calls=%fused_computation | custom fusion | bytes 6292224 | tf_op jit(solution)/shard_map/gather | solution.py:38
  19.1 0.0 copy-done.1
  19.1 9.7 %gather_fusion.1 = bf16[192,4,2048]{2,1,0:T(4,128)(2,1)} fusion(bf16[16,4,2048]{2,1,0:T(4,128)(2,1)S(1)} %copy-done.1, s32[1024]{0:T(1024)S(1)} %pad_clamp_fusion), kind=kCustom, calls=%fused_computation.1 | custom fusion | bytes 6292224 | tf_op jit(solution)/shard_map/gather | solution.py:39
  28.8 9.7 %multiply_reduce_fusion = f32[192,2048]{1,0:T(8,128)S(1)} fusion(bf16[192,4,2048]{2,1,0:T(4,128)(2,1)} %gather_fusion.1, bf16[192,4,2048]{2,1,0:T(4,128)(2,1)} %gather_fusion, f32[192,4]{1,0:T(8,128)S(1)} %copy.10), kind=kLoop, calls=%fused_computation.2 | loop fusion | flops 7471104 | bytes 7867392 | tf_op jit(solution)/shard_map/reduce_sum | solution.py:40
  38.5 0.0 copy-start.3
  38.5 1.0 multiply_convert_fusion
  39.5 0.0 all-gather.4.cloned.1.call-update
  39.5 0.0 all-gather.6.cloned.1.call-start
  39.6 1.4 copy.14
  41.0 4.9 %collective-permute-start = (bf16[192,2,128]{0,2,1:T(8,128)(2,1)S(1)}, bf16[192,2,128]{0,2,1:T(8,128)(2,1)S(1)}, u32[]{:S(2)}, u32[]{:S(2)}) collective-permute-start(bf16[192,2,128]{0,2,1:T(8,128)(2,1)S(1)} %get-tuple-element.2), channel_id=1, source_target_pairs={{0,4},{4,8},{8,12},{12,16},{16,20},{20,24},{24,28},{1,5},{5,9},{9,... | collective-permute-start | bytes 294920 | tf_op jit(solution)/shard_map/ppermute | solution.py:19
  46.0 1.3 collective-permute-start.1
  47.3 0.0 copy-done.3
  47.3 7.1 %all_gather.13 = bf16[768,256]{1,0:T(8,128)(2,1)S(1)} all-gather(bf16[192,256]{1,0:T(8,128)(2,1)S(1)} %copy-done.3), channel_id=1, replica_groups=mesh['mp'=8,'dp'=4] {'dp'}, dimensions={0}, use_global_device_ids=true | all-gather | bytes 491520 | tf_op jit(solution)/shard_map/all_gather | solution.py:54
  54.4 0.0 collective-permute-done
  54.4 0.0 collective-permute-done.1
  54.4 0.3 maximum_convert_fusion
  54.7 0.2 slice.54
  54.9 1.0 fusion.5
  55.9 0.1 slice.57
  56.1 0.8 fusion.11
  56.9 14.4 %all-gather.4.cloned.1.call-done = bf16[768,2048]{1,0:T(8,128)(2,1)} async-done(((bf16[192,2048]{1,0:T(8,128)(2,1)}), bf16[768,2048]{1,0:T(8,128)(2,1)}) %all-gather.4.cloned.1.call-update) | async-done | bytes 3145744 | tf_op jit(solution)/shard_map/all_gather | solution.py:57
  71.3 3.1 %fusion.13 = f32[192,768]{1,0:T(8,128)S(1)} fusion(bf16[192,2048]{0,1:T(8,128)(2,1)S(1)} %bitcast.11, bf16[768,2048]{1,0:T(8,128)(2,1)} %all-gather.4.cloned.1.call-done), kind=kOutput, calls=%fused_computation.31 | convolution fusion | flops 603979776 | bytes 4521984 | tf_op jit(solution)/shard_map/dot_general | solution.py:55
  74.4 1.1 fusion.14
  75.5 0.0 all-gather.6.cloned.1.call-update
  75.5 0.0 reduce-scatter.2.cloned.1.call-start
  75.6 45.7 %all-gather.6.cloned.1.call-done = f32[1536,256]{1,0:T(8,128)} async-done(((f32[192,256]{1,0:T(8,128)}), f32[1536,256]{1,0:T(8,128)}) %all-gather.6.cloned.1.call-update) | async-done | bytes 1572880 | tf_op jit(solution)/shard_map/all_gather | solution.py:66
  121.3 1.5 reduce_sum.19
  122.9 0.0 copy-start.2
  122.9 1.8 %fusion.15 = f32[2048,256]{1,0:T(8,128)} fusion(bf16[192,2048]{0,1:T(8,128)(2,1)S(1)} %bitcast.12, bf16[192,256]{1,0:T(8,128)(2,1)S(1)} %add_convert_fusion), kind=kOutput, calls=%fused_computation.33 | convolution fusion | flops 201326592 | bytes 2981888 | tf_op jit(solution)/shard_map/dot_general | solution.py:71
  124.7 0.0 reduce-scatter.2.cloned.1.call-update
  124.7 0.0 copy-done.2
  124.7 29.7 %reduce-scatter.2.cloned.1.call-done = f32[512,256]{1,0:T(8,128)} async-done(((f32[2048,256]{1,0:T(8,128)}), f32[512,256]{1,0:T(8,128)}) %reduce-scatter.2.cloned.1.call-update) | async-done | bytes 524304 | tf_op jit(solution)/shard_map/reduce_scatter | solution.py:70
  154.4 1.9 %broadcast_multiply_fusion = f32[512,256]{1,0:T(8,128)} fusion(f32[512,256]{1,0:T(8,128)} %reduce-scatter.2.cloned.1.call-done), kind=kLoop, calls=%fused_computation.23 | loop fusion | flops 131072 | bytes 1048576 | tf_op jit(solution)/shard_map/div | solution.py:78
  (5 shorter events, 0.1 us)
Async XLA Ops:
  7.2 2.3 %copy-start = (bf16[64,4,2048]{2,1,0:T(4,128)(2,1)S(1)}, bf16[64,4,2048]{2,1,0:T(4,128)(2,1)}, u32[]{:S(2)}) copy-start(bf16[64,4,2048]{2,1,0:T(4,128)(2,1)} %param.7) | copy-start | bytes 3145732
  7.2 64.1 %all-gather.4.cloned.1.call-start = ((), (), s32[]{:S(2)}) async-start(), calls=%async_computation.1 | async-start | bytes 3932160 | tf_op jit(solution)/shard_map/all_gather | solution.py:57
  9.5 9.6 %copy-start.1 = (bf16[16,4,2048]{2,1,0:T(4,128)(2,1)S(1)}, bf16[16,4,2048]{2,1,0:T(4,128)(2,1)}, u32[]{:S(2)}) copy-start(bf16[16,4,2048]{2,1,0:T(4,128)(2,1)} %param.6) | copy-start | bytes 786436
  38.5 8.8 %copy-start.3 = (bf16[192,256]{1,0:T(8,128)(2,1)S(1)}, bf16[192,256]{1,0:T(8,128)(2,1)}, u32[]{:S(2)}) copy-start(bf16[192,256]{1,0:T(8,128)(2,1)} %param.11) | copy-start | bytes 294916
  39.5 81.8 %all-gather.6.cloned.1.call-start = ((), (), s32[]{:S(2)}) async-start(), calls=%async_computation.3 | async-start | bytes 1769472 | tf_op jit(solution)/shard_map/all_gather | solution.py:66
  41.0 13.3 %collective-permute-start = (bf16[192,2,128]{0,2,1:T(8,128)(2,1)S(1)}, bf16[192,2,128]{0,2,1:T(8,128)(2,1)S(1)}, u32[]{:S(2)}, u32[]{:S(2)}) collective-permute-start(bf16[192,2,128]{0,2,1:T(8,128)(2,1)S(1)} %get-tuple-element.2), channel_id=1, source_target_pairs={{0,4},{4,8},{8,12},{12,16},{16,20},{20,24},{24,28},{1,5},{5,9},{9,... | collective-permute-start | bytes 294920 | tf_op jit(solution)/shard_map/ppermute | solution.py:19
  46.0 8.4 %collective-permute-start.1 = (bf16[192,2,128]{0,2,1:T(8,128)(2,1)S(1)}, bf16[192,2,128]{0,2,1:T(8,128)(2,1)S(1)}, u32[]{:S(2)}, u32[]{:S(2)}) collective-permute-start(bf16[192,2,128]{0,2,1:T(8,128)(2,1)S(1)} %get-tuple-element.3), channel_id=1, source_target_pairs={{4,0},{8,4},{12,8},{16,12},{20,16},{24,20},{28,24},{5,1},{9,5},{13... | collective-permute-start | bytes 294920 | tf_op jit(solution)/shard_map/ppermute | solution.py:20
  75.5 78.8 %reduce-scatter.2.cloned.1.call-start = ((), (), s32[]{:S(2)}) async-start(), calls=%async_computation.2 | async-start | bytes 2621440 | tf_op jit(solution)/shard_map/reduce_scatter | solution.py:70
  122.9 1.8 %copy-start.2 = (bf16[192,256]{1,0:T(8,128)(2,1)}, bf16[192,256]{1,0:T(8,128)(2,1)S(1)}, u32[]{:S(2)}) copy-start(bf16[192,256]{1,0:T(8,128)(2,1)S(1)} %add_convert_fusion) | copy-start | bytes 294916
Sparse Core Ops, SparseCore 0:
  39.6 31.6 all-gather.3
  75.7 45.6 all-gather.5
  124.8 29.5 reduce-scatter.1
